TPU v7x, 32 devices: a whole 2x2x4 slice. The times are simulated.
32 devices in a mesh: corpus: 4 (over y, x), fsdp: 8 (over z, core).
Axes of the slice: x: 2, y: 2, z: 4, core: 2. Of those that a mesh axis runs over, the one named last changes fastest.
Arguments:
- inputs: bfloat16 [2048, 4096], P('fsdp', 'corpus'), may hold values from -128 to 128
- norm_gain: float32 [4096], replicated, may hold values from 0.1 to 1.9
- w_query: bfloat16 [4096, 8192], P('fsdp', 'corpus'), may hold values from -0.09375 to 0.09375
- w_key: bfloat16 [4096, 1024], P('fsdp', 'corpus'), may hold values from -0.09375 to 0.09375
- w_value: bfloat16 [4096, 1024], P('fsdp', 'corpus'), may hold values from -0.375 to 0.375
- query_bias: float32 [8192], P('corpus'), may hold values from -16 to 16
- key_bias: float32 [1024], P('corpus'), may hold values from -16 to 16
- value_bias: float32 [1024], P('corpus'), may hold values from -4 to 4
- key_cache: bfloat16 [8, 2048, 1024], P('fsdp', None, 'corpus'), may hold values from -16 to 16
- value_cache: bfloat16 [8, 2048, 1024], P('fsdp', None, 'corpus'), may hold values from -16 to 16
- source_doc: int32 [32], P('fsdp'), may hold values from 0 to 7, as said below
- prefix_len: int32 [32], P('fsdp'), may hold values from 1 to 2048
Outputs:
- attention: bfloat16 [2048, 8192], P('fsdp', 'corpus')
Inputs may be any that keep to these rules, and one draw needn't show every extreme that they name: `source_doc`: within the suffixes of one index of fsdp (aligned blocks of 4) no document appears more than 2 times, and one document, drawn from the seed, appears exactly 2 times in every such block.
All inputs are finite; a program needn't handle non-finite values.
Results may differ from a plain program's by a relative error of at most 0.0075.
The roundings to bfloat16 on the way count: a program that leaves them out, or rounds other values in their place, can miss the bound.
Values may be sent and summed in bfloat16 or wider, within the bound.
A program may use at most 128 MiB of HBM per device.

v0:
```python
import jax
import jax.numpy as jnp
from jax import lax
from jax.sharding import PartitionSpec as P

HD = 128
SL = 64
CAP = 2
EPS = 1e-06
THETA = 1000000.0
MASKED = -1e30


def rope_tables(position, width):
    half = width // 2
    freq = THETA ** (-(jnp.arange(half, dtype=jnp.float32) * 2.0 / width))
    angle = position.astype(jnp.float32)[..., None] * freq
    angle = jnp.concatenate([angle, angle], axis=-1)
    return (jnp.cos(angle), jnp.sin(angle))


def rotate(vector, cosine, sine):
    half = vector.shape[-1] // 2
    turned = jnp.concatenate([-vector[..., half:], vector[..., :half]], axis=-1)
    return vector * cosine + turned * sine


def normalize(rows, norm_gain):
    wide = rows.astype(jnp.float32)
    spread = jnp.mean(wide * wide, axis=-1, keepdims=True)
    return (wide * lax.rsqrt(spread + EPS) * norm_gain).astype(jnp.bfloat16)


def partial_attend(query, keys, values, live):
    count = query.shape[0]
    width = query.shape[2]
    length = keys.shape[0]
    kv_heads = keys.shape[1] // width
    group = query.shape[1] // kv_heads
    grouped = query.reshape(count, kv_heads, group, width)
    key_rows = keys.reshape(length, kv_heads, width)
    scores = jnp.einsum(
        "tkgd,lkd->tkgl", grouped, key_rows, preferred_element_type=jnp.float32
    ) * width ** (-0.5)
    scores = jnp.where(live[:, None, None, :], scores, MASKED)
    peak = jnp.max(scores, axis=-1)
    weights = jnp.exp(scores - peak[..., None])
    total = jnp.sum(weights, axis=-1)
    rounded = weights.astype(jnp.bfloat16)
    value_rows = values.reshape(length, kv_heads, width)
    weighted = jnp.einsum("tkgl,lkd->tkgd", rounded, value_rows, preferred_element_type=jnp.float32)
    return (
        weighted.reshape(count, kv_heads * group * width),
        peak.reshape(count, kv_heads * group),
        total.reshape(count, kv_heads * group),
    )


def settle(part):
    weighted, peak, total = part
    shape = peak.shape + (-1,)
    normed = (
        (weighted.reshape(shape) / total[..., None]).reshape(weighted.shape).astype(jnp.bfloat16)
    )
    return (normed, peak + jnp.log(total))


def combine(prefix_normed, prefix_lse, own):
    own_out, own_peak, own_total = own
    top = jnp.maximum(prefix_lse, own_peak)
    scale_first = jnp.exp(prefix_lse - top)
    scale_second = jnp.exp(own_peak - top)
    divisor = scale_first + own_total * scale_second
    shape = own_peak.shape + (-1,)
    mixed = (
        prefix_normed.astype(jnp.float32).reshape(shape) * scale_first[..., None]
        + own_out.reshape(shape) * scale_second[..., None]
    )
    mixed = mixed / divisor[..., None]
    return mixed.reshape(own_peak.shape[:-1] + (-1,)).astype(jnp.bfloat16)


def shards(
    inputs,
    norm_gain,
    w_query,
    w_key,
    w_value,
    query_bias,
    key_bias,
    value_bias,
    key_cache,
    value_cache,
    source_doc,
    prefix_len,
):
    full_rows = lax.all_gather(inputs, "corpus", axis=1, tiled=True)
    normed = normalize(full_rows, norm_gain)
    query_lin = jnp.dot(
        normed,
        lax.all_gather(w_query, "fsdp", axis=0, tiled=True),
        preferred_element_type=jnp.float32,
    )
    key_lin = jnp.dot(
        normed,
        lax.all_gather(w_key, "fsdp", axis=0, tiled=True),
        preferred_element_type=jnp.float32,
    )
    value_lin = jnp.dot(
        normed,
        lax.all_gather(w_value, "fsdp", axis=0, tiled=True),
        preferred_element_type=jnp.float32,
    )
    suffixes = source_doc.shape[0]
    width = HD
    q_heads = w_query.shape[1] // width
    kv_heads = w_key.shape[1] // width
    position = prefix_len[:, None] + jnp.arange(SL, dtype=jnp.int32)[None, :]
    cosine, sine = rope_tables(position, width)
    cosine = cosine[:, :, None, :]
    sine = sine[:, :, None, :]
    queries = rotate(
        (query_lin + query_bias).reshape(suffixes, SL, q_heads, width), cosine, sine
    ).astype(jnp.bfloat16)
    own_keys = rotate(
        (key_lin + key_bias).reshape(suffixes, SL, kv_heads, width), cosine, sine
    ).astype(jnp.bfloat16)
    own_keys = own_keys.reshape(suffixes, SL, kv_heads * width)
    own_values = (
        (value_lin + value_bias).astype(jnp.bfloat16).reshape(suffixes, SL, kv_heads * width)
    )
    causal = jnp.arange(SL, dtype=jnp.int32)[None, :] <= jnp.arange(SL, dtype=jnp.int32)[:, None]
    own_part = jax.vmap(partial_attend, in_axes=(0, 0, 0, None))(
        queries, own_keys, own_values, causal
    )
    documents = lax.axis_size("fsdp")
    slots = documents * CAP
    doc_length = key_cache.shape[1]
    order = jnp.arange(suffixes, dtype=jnp.int32)
    earlier = (source_doc[None, :] == source_doc[:, None]) & (order[None, :] < order[:, None])
    ranking = jnp.sum(earlier.astype(jnp.int32), axis=1)
    slot_of = source_doc * CAP + ranking
    matches = slot_of[None, :] == jnp.arange(slots, dtype=jnp.int32)[:, None]
    holder = jnp.sum(jnp.where(matches, order[None, :], 0), axis=1)
    occupied = jnp.any(matches, axis=1)
    slot_length = jnp.where(occupied, jnp.take(prefix_len, holder, axis=0), 0)
    slot_mask = (jnp.arange(doc_length, dtype=jnp.int32)[None, :] < slot_length[:, None]).astype(
        jnp.bfloat16
    )
    slot_queries = jnp.take(queries, holder, axis=0)
    initial = (
        jnp.zeros((suffixes, SL, q_heads * width), jnp.float32),
        jnp.zeros((suffixes, SL, q_heads), jnp.float32),
        jnp.zeros((suffixes, SL, q_heads), jnp.float32),
    )
    key_piece = lax.all_gather(key_cache, "fsdp", axis=0, tiled=True)
    value_piece = lax.all_gather(value_cache, "fsdp", axis=0, tiled=True)
    count = key_piece.shape[0]

    def one_document(item):
        doc_queries, doc_masks, doc_keys, doc_values = item
        live = jnp.broadcast_to(doc_masks[:, None, :] > 0, (CAP, SL, doc_masks.shape[-1]))
        return jax.vmap(partial_attend, in_axes=(0, None, None, 0))(
            doc_queries, doc_keys, doc_values, live
        )

    results = lax.map(
        one_document,
        (
            slot_queries.reshape((count, CAP) + slot_queries.shape[1:]),
            slot_mask.reshape(count, CAP, doc_length),
            key_piece,
            value_piece,
        ),
    )
    results = tuple((part.reshape((count * CAP,) + part.shape[2:]) for part in results))
    inside = (slot_of >= 0) & (slot_of < count * CAP)
    chosen = jnp.clip(slot_of, 0, count * CAP - 1)
    gathered_part = tuple(
        (
            jnp.where(inside[:, None, None], jnp.take(fresh, chosen, axis=0), older)
            for older, fresh in zip(initial, results)
        )
    )
    prefix_normed, prefix_lse = settle(gathered_part)
    attention = combine(prefix_normed, prefix_lse, own_part)
    return attention.reshape(suffixes * SL, q_heads * width)


def solution(mesh):
    in_specs = (
        P("fsdp", "corpus"),
        P(),
        P("fsdp", "corpus"),
        P("fsdp", "corpus"),
        P("fsdp", "corpus"),
        P("corpus"),
        P("corpus"),
        P("corpus"),
        P("fsdp", None, "corpus"),
        P("fsdp", None, "corpus"),
        P("fsdp"),
        P("fsdp"),
    )
    out_specs = P("fsdp", "corpus")
    return jax.shard_map(shards, mesh=mesh, in_specs=in_specs, out_specs=out_specs, check_vma=False)
```

profile of v0, /device:TPU:0, one launch (start us, length us, event | category | flops | bytes accessed | tf_op | source)
XLA Modules:
  0.0 685.7 jit_solution(6007420988527938023)
XLA Ops:
  15.4 31.9 %all-gather.11.cloned.1.call-done = bf16[256,4096]{1,0:T(8,128)(2,1)} async-done(((bf16[256,1024]{1,0:T(8,128)(2,1)}), bf16[256,4096]{1,0:T(8,128)(2,1)}) %all-gather.11.cloned.1.call-update) | async-done | bytes 2097168 | tf_op jit(solution)/shard_map/all_gather | solution.py:97
  47.3 2.2 fusion.13
  49.5 28.5 %all-gather.15.cloned.1.call-done = bf16[4096,256]{1,0:T(8,128)(2,1)} async-done(((bf16[512,256]{1,0:T(8,128)(2,1)}), bf16[4096,256]{1,0:T(8,128)(2,1)}) %all-gather.15.cloned.1.call-update) | async-done | bytes 2097168 | tf_op jit(solution)/shard_map/all_gather | solution.py:106
  78.0 2.4 convolution_add_fusion.2
  80.5 27.7 %all-gather.17.cloned.1.call-done = bf16[4096,256]{1,0:T(8,128)(2,1)} async-done(((bf16[512,256]{1,0:T(8,128)(2,1)}), bf16[4096,256]{1,0:T(8,128)(2,1)}) %all-gather.17.cloned.1.call-update) | async-done | bytes 2097168 | tf_op jit(solution)/shard_map/all_gather | solution.py:111
  108.2 2.4 fusion.27
  110.8 149.5 %all-gather.13.cloned.1.call-done = bf16[4096,2048]{1,0:T(8,128)(2,1)} async-done(((bf16[512,2048]{1,0:T(8,128)(2,1)}), bf16[4096,2048]{1,0:T(8,128)(2,1)}) %all-gather.13.cloned.1.call-update) | async-done | bytes 16777232 | tf_op jit(solution)/shard_map/all_gather | solution.py:101
  260.3 8.2 %fusion.26 = f32[32,8,16,128]{3,1,2,0:T(8,128)S(1)} fusion(bf16[4096,2048]{1,0:T(8,128)(2,1)} %all-gather.13.cloned.1.call-done, f32[2048]{0:T(1024)S(1)} %copy-done.18, bf16[256,4096]{1,0:T(8,128)(2,1)S(1)} %copy-done.7, f32[4096]{0:T(1024)S(1)} %copy-done.17, f32[256]{0:T(256)S(1)} %add_rsqrt_fusion), kind=kOutput, calls=%fused_computation.52 | convolution fusion | flops 4299685888 | bytes 20997120 | tf_op jit(solution)/shard_map/dot_general | solution.py:99
  272.3 1.6 fusion.56
  275.3 2.5 copy.105
  277.8 2.7 reshape.216
  280.5 3.0 fusion.20
  283.5 3.0 gather_fusion.1
  287.0 4.6 broadcast_select_fusion
  291.7 50.4 %all-gather.9.cloned.1.call-done = bf16[8,2048,256]{2,1,0:T(8,128)(2,1)} async-done(((bf16[1,2048,256]{2,1,0:T(8,128)(2,1)}), bf16[8,2048,256]{2,1,0:T(8,128)(2,1)}) %all-gather.9.cloned.1.call-update) | async-done | bytes 8388624 | tf_op jit(solution)/shard_map/all_gather | solution.py:156
  342.1 82.1 %all-gather.7.cloned.1.call-done = bf16[8,2048,256]{2,1,0:T(8,128)(2,1)} async-done(((bf16[1,2048,256]{2,1,0:T(8,128)(2,1)}), bf16[8,2048,256]{2,1,0:T(8,128)(2,1)}) %all-gather.7.cloned.1.call-update) | async-done | bytes 8388624 | tf_op jit(solution)/shard_map/all_gather | solution.py:157
  424.2 241.4 %while.14 = (s32[]{:T(128)}, f32[8,2,64,2048]{3,2,1,0:T(8,128)}, f32[8,2,64,16]{2,3,1,0:T(8,128)S(1)}, f32[8,2,64,16]{2,3,1,0:T(8,128)S(1)}, bf16[8,2048,256]{2,...) while((s32[]{:T(128)}, f32[8,2,64,2048]{3,2,1,0:T(8,128)}, ...), condition=%wide.region_7.8_spmd, body=%wide.region_4.0_spmd.sunk | while | flops 2193620992 | bytes 74047632 | solution.py:167
  427.2 1.3 constant_dynamic-slice_fusion.4
  428.5 1.4 copy.160
  429.9 7.1 %fusion.71 = (f32[2,64,2,8]{1,3,0,2:T(8,128)S(1)}, f32[2,2048,2,64,8]{1,3,4,2,0:T(8,128)}) fusion(pred[2,2048]{1,0:T(4,128)(4,1)S(1)} %compare_bitcast_fusion.2, bf16[2048,2,128,1,1]{0,2,4,3,1:T(8,128)(2,1)S(1)} %bitcast.138, bf16[2,64,2,8,128]{4,3,2,1,0:T(8,128)(2,1)S(1)} %dynamic-slice_bitcast_fusion.2), kind=kOutput, calls=%fused_computation.9.clone.1 | convolution fusion | flops 1086322688 | bytes 18362368 | tf_op jit(solution)/shard_map/while/body/eval_jaxpr/vmap(tkgd,lkd->tkgl)/dot_general | solution.py:42
  437.1 7.6 %fusion.72 = f32[2,64,2,8,128]{4,1,3,0,2:T(8,128)S(1)} fusion(bf16[2048,2,128,1,1]{0,2,4,3,1:T(8,128)(2,1)S(1)} %bitcast.142, f32[2,2048,2,64,8]{1,3,4,2,0:T(8,128)} %get-tuple-element.168, f32[2,64,2,8]{1,3,0,2:T(8,128)S(1)} %get-tuple-element.169, pred[2,2048]{1,0:T(4,128)(4,1)S(1)} %compare_bitcast_fusion.2), kind=kOutput, calls=%fused_computation.12.clone.1 | convolution fusion | flops 1090519040 | bytes 18886656 | tf_op jit(solution)/shard_map/while/body/eval_jaxpr/vmap(tkgl,lkd->tkgd)/dot_general | solution.py:51
  444.6 7.8 %fusion.73 = f32[2,64,2,8]{1,3,0,2:T(8,128)S(1)} fusion(f32[2,2048,2,64,8]{1,3,4,2,0:T(8,128)} %get-tuple-element.168, f32[2,64,2,8]{1,3,0,2:T(8,128)S(1)} %get-tuple-element.169, pred[2,2048]{1,0:T(4,128)(4,1)S(1)} %compare_bitcast_fusion.2), kind=kLoop, calls=%fused_computation.7.clone.1 | loop fusion | flops 16775168 | bytes 16797696 | tf_op jit(solution)/shard_map/while/body/eval_jaxpr/vmap()/reduce_sum | solution.py:48
  455.4 1.3 constant_dynamic-slice_fusion.5
  457.4 1.3 constant_dynamic-slice_fusion.4
  458.7 1.4 copy.160
  460.1 7.1 %fusion.71 = (f32[2,64,2,8]{1,3,0,2:T(8,128)S(1)}, f32[2,2048,2,64,8]{1,3,4,2,0:T(8,128)}) fusion(pred[2,2048]{1,0:T(4,128)(4,1)S(1)} %compare_bitcast_fusion.2, bf16[2048,2,128,1,1]{0,2,4,3,1:T(8,128)(2,1)S(1)} %bitcast.138, bf16[2,64,2,8,128]{4,3,2,1,0:T(8,128)(2,1)S(1)} %dynamic-slice_bitcast_fusion.2), kind=kOutput, calls=%fused_computation.9.clone.1 | convolution fusion | flops 1086322688 | bytes 18362368 | tf_op jit(solution)/shard_map/while/body/eval_jaxpr/vmap(tkgd,lkd->tkgl)/dot_general | solution.py:42
  467.2 7.6 %fusion.72 = f32[2,64,2,8,128]{4,1,3,0,2:T(8,128)S(1)} fusion(bf16[2048,2,128,1,1]{0,2,4,3,1:T(8,128)(2,1)S(1)} %bitcast.142, f32[2,2048,2,64,8]{1,3,4,2,0:T(8,128)} %get-tuple-element.168, f32[2,64,2,8]{1,3,0,2:T(8,128)S(1)} %get-tuple-element.169, pred[2,2048]{1,0:T(4,128)(4,1)S(1)} %compare_bitcast_fusion.2), kind=kOutput, calls=%fused_computation.12.clone.1 | convolution fusion | flops 1090519040 | bytes 18886656 | tf_op jit(solution)/shard_map/while/body/eval_jaxpr/vmap(tkgl,lkd->tkgd)/dot_general | solution.py:51
  474.8 7.8 %fusion.73 = f32[2,64,2,8]{1,3,0,2:T(8,128)S(1)} fusion(f32[2,2048,2,64,8]{1,3,4,2,0:T(8,128)} %get-tuple-element.168, f32[2,64,2,8]{1,3,0,2:T(8,128)S(1)} %get-tuple-element.169, pred[2,2048]{1,0:T(4,128)(4,1)S(1)} %compare_bitcast_fusion.2), kind=kLoop, calls=%fused_computation.7.clone.1 | loop fusion | flops 16775168 | bytes 16797696 | tf_op jit(solution)/shard_map/while/body/eval_jaxpr/vmap()/reduce_sum | solution.py:48
  485.6 1.3 constant_dynamic-slice_fusion.5
  488.8 1.4 copy.160
  490.3 7.1 %fusion.71 = (f32[2,64,2,8]{1,3,0,2:T(8,128)S(1)}, f32[2,2048,2,64,8]{1,3,4,2,0:T(8,128)}) fusion(pred[2,2048]{1,0:T(4,128)(4,1)S(1)} %compare_bitcast_fusion.2, bf16[2048,2,128,1,1]{0,2,4,3,1:T(8,128)(2,1)S(1)} %bitcast.138, bf16[2,64,2,8,128]{4,3,2,1,0:T(8,128)(2,1)S(1)} %dynamic-slice_bitcast_fusion.2), kind=kOutput, calls=%fused_computation.9.clone.1 | convolution fusion | flops 1086322688 | bytes 18362368 | tf_op jit(solution)/shard_map/while/body/eval_jaxpr/vmap(tkgd,lkd->tkgl)/dot_general | solution.py:42
  497.4 7.6 %fusion.72 = f32[2,64,2,8,128]{4,1,3,0,2:T(8,128)S(1)} fusion(bf16[2048,2,128,1,1]{0,2,4,3,1:T(8,128)(2,1)S(1)} %bitcast.142, f32[2,2048,2,64,8]{1,3,4,2,0:T(8,128)} %get-tuple-element.168, f32[2,64,2,8]{1,3,0,2:T(8,128)S(1)} %get-tuple-element.169, pred[2,2048]{1,0:T(4,128)(4,1)S(1)} %compare_bitcast_fusion.2), kind=kOutput, calls=%fused_computation.12.clone.1 | convolution fusion | flops 1090519040 | bytes 18886656 | tf_op jit(solution)/shard_map/while/body/eval_jaxpr/vmap(tkgl,lkd->tkgd)/dot_general | solution.py:51
  505.0 7.8 %fusion.73 = f32[2,64,2,8]{1,3,0,2:T(8,128)S(1)} fusion(f32[2,2048,2,64,8]{1,3,4,2,0:T(8,128)} %get-tuple-element.168, f32[2,64,2,8]{1,3,0,2:T(8,128)S(1)} %get-tuple-element.169, pred[2,2048]{1,0:T(4,128)(4,1)S(1)} %compare_bitcast_fusion.2), kind=kLoop, calls=%fused_computation.7.clone.1 | loop fusion | flops 16775168 | bytes 16797696 | tf_op jit(solution)/shard_map/while/body/eval_jaxpr/vmap()/reduce_sum | solution.py:48
  515.8 1.3 constant_dynamic-slice_fusion.5
  517.7 1.3 constant_dynamic-slice_fusion.4
  519.0 1.4 copy.160
  520.4 7.1 %fusion.71 = (f32[2,64,2,8]{1,3,0,2:T(8,128)S(1)}, f32[2,2048,2,64,8]{1,3,4,2,0:T(8,128)}) fusion(pred[2,2048]{1,0:T(4,128)(4,1)S(1)} %compare_bitcast_fusion.2, bf16[2048,2,128,1,1]{0,2,4,3,1:T(8,128)(2,1)S(1)} %bitcast.138, bf16[2,64,2,8,128]{4,3,2,1,0:T(8,128)(2,1)S(1)} %dynamic-slice_bitcast_fusion.2), kind=kOutput, calls=%fused_computation.9.clone.1 | convolution fusion | flops 1086322688 | bytes 18362368 | tf_op jit(solution)/shard_map/while/body/eval_jaxpr/vmap(tkgd,lkd->tkgl)/dot_general | solution.py:42
  527.6 7.6 %fusion.72 = f32[2,64,2,8,128]{4,1,3,0,2:T(8,128)S(1)} fusion(bf16[2048,2,128,1,1]{0,2,4,3,1:T(8,128)(2,1)S(1)} %bitcast.142, f32[2,2048,2,64,8]{1,3,4,2,0:T(8,128)} %get-tuple-element.168, f32[2,64,2,8]{1,3,0,2:T(8,128)S(1)} %get-tuple-element.169, pred[2,2048]{1,0:T(4,128)(4,1)S(1)} %compare_bitcast_fusion.2), kind=kOutput, calls=%fused_computation.12.clone.1 | convolution fusion | flops 1090519040 | bytes 18886656 | tf_op jit(solution)/shard_map/while/body/eval_jaxpr/vmap(tkgl,lkd->tkgd)/dot_general | solution.py:51
  535.1 7.8 %fusion.73 = f32[2,64,2,8]{1,3,0,2:T(8,128)S(1)} fusion(f32[2,2048,2,64,8]{1,3,4,2,0:T(8,128)} %get-tuple-element.168, f32[2,64,2,8]{1,3,0,2:T(8,128)S(1)} %get-tuple-element.169, pred[2,2048]{1,0:T(4,128)(4,1)S(1)} %compare_bitcast_fusion.2), kind=kLoop, calls=%fused_computation.7.clone.1 | loop fusion | flops 16775168 | bytes 16797696 | tf_op jit(solution)/shard_map/while/body/eval_jaxpr/vmap()/reduce_sum | solution.py:48
  545.9 1.3 constant_dynamic-slice_fusion.5
  547.9 1.3 constant_dynamic-slice_fusion.4
  549.2 1.4 copy.160
  550.6 7.1 %fusion.71 = (f32[2,64,2,8]{1,3,0,2:T(8,128)S(1)}, f32[2,2048,2,64,8]{1,3,4,2,0:T(8,128)}) fusion(pred[2,2048]{1,0:T(4,128)(4,1)S(1)} %compare_bitcast_fusion.2, bf16[2048,2,128,1,1]{0,2,4,3,1:T(8,128)(2,1)S(1)} %bitcast.138, bf16[2,64,2,8,128]{4,3,2,1,0:T(8,128)(2,1)S(1)} %dynamic-slice_bitcast_fusion.2), kind=kOutput, calls=%fused_computation.9.clone.1 | convolution fusion | flops 1086322688 | bytes 18362368 | tf_op jit(solution)/shard_map/while/body/eval_jaxpr/vmap(tkgd,lkd->tkgl)/dot_general | solution.py:42
  557.7 7.6 %fusion.72 = f32[2,64,2,8,128]{4,1,3,0,2:T(8,128)S(1)} fusion(bf16[2048,2,128,1,1]{0,2,4,3,1:T(8,128)(2,1)S(1)} %bitcast.142, f32[2,2048,2,64,8]{1,3,4,2,0:T(8,128)} %get-tuple-element.168, f32[2,64,2,8]{1,3,0,2:T(8,128)S(1)} %get-tuple-element.169, pred[2,2048]{1,0:T(4,128)(4,1)S(1)} %compare_bitcast_fusion.2), kind=kOutput, calls=%fused_computation.12.clone.1 | convolution fusion | flops 1090519040 | bytes 18886656 | tf_op jit(solution)/shard_map/while/body/eval_jaxpr/vmap(tkgl,lkd->tkgd)/dot_general | solution.py:51
  565.3 7.8 %fusion.73 = f32[2,64,2,8]{1,3,0,2:T(8,128)S(1)} fusion(f32[2,2048,2,64,8]{1,3,4,2,0:T(8,128)} %get-tuple-element.168, f32[2,64,2,8]{1,3,0,2:T(8,128)S(1)} %get-tuple-element.169, pred[2,2048]{1,0:T(4,128)(4,1)S(1)} %compare_bitcast_fusion.2), kind=kLoop, calls=%fused_computation.7.clone.1 | loop fusion | flops 16775168 | bytes 16797696 | tf_op jit(solution)/shard_map/while/body/eval_jaxpr/vmap()/reduce_sum | solution.py:48
  576.1 1.3 constant_dynamic-slice_fusion.5
  578.1 1.3 constant_dynamic-slice_fusion.4
  579.4 1.4 copy.160
  580.8 7.1 %fusion.71 = (f32[2,64,2,8]{1,3,0,2:T(8,128)S(1)}, f32[2,2048,2,64,8]{1,3,4,2,0:T(8,128)}) fusion(pred[2,2048]{1,0:T(4,128)(4,1)S(1)} %compare_bitcast_fusion.2, bf16[2048,2,128,1,1]{0,2,4,3,1:T(8,128)(2,1)S(1)} %bitcast.138, bf16[2,64,2,8,128]{4,3,2,1,0:T(8,128)(2,1)S(1)} %dynamic-slice_bitcast_fusion.2), kind=kOutput, calls=%fused_computation.9.clone.1 | convolution fusion | flops 1086322688 | bytes 18362368 | tf_op jit(solution)/shard_map/while/body/eval_jaxpr/vmap(tkgd,lkd->tkgl)/dot_general | solution.py:42
  587.9 7.6 %fusion.72 = f32[2,64,2,8,128]{4,1,3,0,2:T(8,128)S(1)} fusion(bf16[2048,2,128,1,1]{0,2,4,3,1:T(8,128)(2,1)S(1)} %bitcast.142, f32[2,2048,2,64,8]{1,3,4,2,0:T(8,128)} %get-tuple-element.168, f32[2,64,2,8]{1,3,0,2:T(8,128)S(1)} %get-tuple-element.169, pred[2,2048]{1,0:T(4,128)(4,1)S(1)} %compare_bitcast_fusion.2), kind=kOutput, calls=%fused_computation.12.clone.1 | convolution fusion | flops 1090519040 | bytes 18886656 | tf_op jit(solution)/shard_map/while/body/eval_jaxpr/vmap(tkgl,lkd->tkgd)/dot_general | solution.py:51
  595.5 7.8 %fusion.73 = f32[2,64,2,8]{1,3,0,2:T(8,128)S(1)} fusion(f32[2,2048,2,64,8]{1,3,4,2,0:T(8,128)} %get-tuple-element.168, f32[2,64,2,8]{1,3,0,2:T(8,128)S(1)} %get-tuple-element.169, pred[2,2048]{1,0:T(4,128)(4,1)S(1)} %compare_bitcast_fusion.2), kind=kLoop, calls=%fused_computation.7.clone.1 | loop fusion | flops 16775168 | bytes 16797696 | tf_op jit(solution)/shard_map/while/body/eval_jaxpr/vmap()/reduce_sum | solution.py:48
  606.3 1.3 constant_dynamic-slice_fusion.5
  608.2 1.3 constant_dynamic-slice_fusion.4
  609.5 1.4 copy.160
  611.0 7.1 %fusion.71 = (f32[2,64,2,8]{1,3,0,2:T(8,128)S(1)}, f32[2,2048,2,64,8]{1,3,4,2,0:T(8,128)}) fusion(pred[2,2048]{1,0:T(4,128)(4,1)S(1)} %compare_bitcast_fusion.2, bf16[2048,2,128,1,1]{0,2,4,3,1:T(8,128)(2,1)S(1)} %bitcast.138, bf16[2,64,2,8,128]{4,3,2,1,0:T(8,128)(2,1)S(1)} %dynamic-slice_bitcast_fusion.2), kind=kOutput, calls=%fused_computation.9.clone.1 | convolution fusion | flops 1086322688 | bytes 18362368 | tf_op jit(solution)/shard_map/while/body/eval_jaxpr/vmap(tkgd,lkd->tkgl)/dot_general | solution.py:42
  618.1 7.6 %fusion.72 = f32[2,64,2,8,128]{4,1,3,0,2:T(8,128)S(1)} fusion(bf16[2048,2,128,1,1]{0,2,4,3,1:T(8,128)(2,1)S(1)} %bitcast.142, f32[2,2048,2,64,8]{1,3,4,2,0:T(8,128)} %get-tuple-element.168, f32[2,64,2,8]{1,3,0,2:T(8,128)S(1)} %get-tuple-element.169, pred[2,2048]{1,0:T(4,128)(4,1)S(1)} %compare_bitcast_fusion.2), kind=kOutput, calls=%fused_computation.12.clone.1 | convolution fusion | flops 1090519040 | bytes 18886656 | tf_op jit(solution)/shard_map/while/body/eval_jaxpr/vmap(tkgl,lkd->tkgd)/dot_general | solution.py:51
  625.7 7.8 %fusion.73 = f32[2,64,2,8]{1,3,0,2:T(8,128)S(1)} fusion(f32[2,2048,2,64,8]{1,3,4,2,0:T(8,128)} %get-tuple-element.168, f32[2,64,2,8]{1,3,0,2:T(8,128)S(1)} %get-tuple-element.169, pred[2,2048]{1,0:T(4,128)(4,1)S(1)} %compare_bitcast_fusion.2), kind=kLoop, calls=%fused_computation.7.clone.1 | loop fusion | flops 16775168 | bytes 16797696 | tf_op jit(solution)/shard_map/while/body/eval_jaxpr/vmap()/reduce_sum | solution.py:48
  636.4 1.3 constant_dynamic-slice_fusion.5
  639.7 1.4 copy.160
  641.1 7.1 %fusion.71 = (f32[2,64,2,8]{1,3,0,2:T(8,128)S(1)}, f32[2,2048,2,64,8]{1,3,4,2,0:T(8,128)}) fusion(pred[2,2048]{1,0:T(4,128)(4,1)S(1)} %compare_bitcast_fusion.2, bf16[2048,2,128,1,1]{0,2,4,3,1:T(8,128)(2,1)S(1)} %bitcast.138, bf16[2,64,2,8,128]{4,3,2,1,0:T(8,128)(2,1)S(1)} %dynamic-slice_bitcast_fusion.2), kind=kOutput, calls=%fused_computation.9.clone.1 | convolution fusion | flops 1086322688 | bytes 18362368 | tf_op jit(solution)/shard_map/while/body/eval_jaxpr/vmap(tkgd,lkd->tkgl)/dot_general | solution.py:42
  648.2 7.6 %fusion.72 = f32[2,64,2,8,128]{4,1,3,0,2:T(8,128)S(1)} fusion(bf16[2048,2,128,1,1]{0,2,4,3,1:T(8,128)(2,1)S(1)} %bitcast.142, f32[2,2048,2,64,8]{1,3,4,2,0:T(8,128)} %get-tuple-element.168, f32[2,64,2,8]{1,3,0,2:T(8,128)S(1)} %get-tuple-element.169, pred[2,2048]{1,0:T(4,128)(4,1)S(1)} %compare_bitcast_fusion.2), kind=kOutput, calls=%fused_computation.12.clone.1 | convolution fusion | flops 1090519040 | bytes 18886656 | tf_op jit(solution)/shard_map/while/body/eval_jaxpr/vmap(tkgl,lkd->tkgd)/dot_general | solution.py:51
  655.8 7.8 %fusion.73 = f32[2,64,2,8]{1,3,0,2:T(8,128)S(1)} fusion(f32[2,2048,2,64,8]{1,3,4,2,0:T(8,128)} %get-tuple-element.168, f32[2,64,2,8]{1,3,0,2:T(8,128)S(1)} %get-tuple-element.169, pred[2,2048]{1,0:T(4,128)(4,1)S(1)} %compare_bitcast_fusion.2), kind=kLoop, calls=%fused_computation.7.clone.1 | loop fusion | flops 16775168 | bytes 16797696 | tf_op jit(solution)/shard_map/while/body/eval_jaxpr/vmap()/reduce_sum | solution.py:48
  666.2 4.2 gather_fusion.2
  674.5 4.4 fusion.16
  (175 shorter events, 51.9 us)
Async XLA Ops:
  6.5 40.7 %all-gather.11.cloned.1.call-start = ((), (), s32[]{:S(2)}) async-start(), calls=%async_computation.2 | async-start | bytes 2621440 | tf_op jit(solution)/shard_map/all_gather | solution.py:97
  7.3 70.7 %all-gather.15.cloned.1.call-start = ((), (), s32[]{:S(2)}) async-start(), calls=%async_computation.4 | async-start | bytes 2359296 | tf_op jit(solution)/shard_map/all_gather | solution.py:106
  8.0 100.2 %all-gather.17.cloned.1.call-start = ((), (), s32[]{:S(2)}) async-start(), calls=%async_computation.5 | async-start | bytes 2359296 | tf_op jit(solution)/shard_map/all_gather | solution.py:111
  8.7 1.8 copy-start.16
  8.8 4.3 copy-start
  8.8 251.5 %all-gather.13.cloned.1.call-start = ((), (), s32[]{:S(2)}) async-start(), calls=%async_computation.3 | async-start | bytes 18874368 | tf_op jit(solution)/shard_map/all_gather | solution.py:101
  9.3 332.7 %all-gather.9.cloned.1.call-start = ((), (), s32[]{:S(2)}) async-start(), calls=%async_computation.1 | async-start | bytes 9437184 | tf_op jit(solution)/shard_map/all_gather | solution.py:156
  9.9 68.1 %copy-start.17 = (f32[4096]{0:T(1024)S(1)}, f32[4096]{0:T(1024)}, u32[]{:S(2)}) copy-start(f32[4096]{0:T(1024)} %param.17) | copy-start | bytes 49156
  9.9 68.1 %copy-start.19 = (f32[256]{0:T(256)S(1)}, f32[256]{0:T(256)}, u32[]{:S(2)}) copy-start(f32[256]{0:T(256)} %param.22) | copy-start | bytes 3076
  9.9 414.2 %all-gather.7.cloned.1.call-start = ((), (), s32[]{:S(2)}) async-start(), calls=%async_computation | async-start | bytes 9437184 | tf_op jit(solution)/shard_map/all_gather | solution.py:157
  10.8 0.5 copy-start.10
  12.2 3.2 copy-start.14
  47.3 30.7 %copy-start.7 = (bf16[256,4096]{1,0:T(8,128)(2,1)S(1)}, bf16[256,4096]{1,0:T(8,128)(2,1)}, u32[]{:S(2)}) copy-start(bf16[256,4096]{1,0:T(8,128)(2,1)} %all-gather.11.cloned.1.call-done) | copy-start | bytes 6291460
  49.5 58.7 %copy-start.20 = (f32[256]{0:T(256)S(1)}, f32[256]{0:T(256)}, u32[]{:S(2)}) copy-start(f32[256]{0:T(256)} %param.23) | copy-start | bytes 3076
  80.5 179.8 %copy-start.18 = (f32[2048]{0:T(1024)S(1)}, f32[2048]{0:T(1024)}, u32[]{:S(2)}) copy-start(f32[2048]{0:T(1024)} %param.21) | copy-start | bytes 24580
  269.6 1.3 copy-start.4
  269.6 2.0 copy-start.5
  273.9 1.4 copy-start.2
  283.5 3.0 copy-start.3
  287.0 137.1 %copy-start.8 = (f32[8,2,64,16]{2,3,1,0:T(8,128)S(1)}, f32[8,2,64,16]{2,3,1,0:T(8,128)}, u32[]{:S(2)}) copy-start(f32[8,2,64,16]{2,3,1,0:T(8,128)} %custom-call.12) | copy-start | bytes 196612
  287.0 137.1 %copy-start.9 = (f32[8,2,64,16]{2,3,1,0:T(8,128)S(1)}, f32[8,2,64,16]{2,3,1,0:T(8,128)}, u32[]{:S(2)}) copy-start(f32[8,2,64,16]{2,3,1,0:T(8,128)} %custom-call.11) | copy-start | bytes 196612
  429.9 7.1 %copy-start.1 = (bf16[1,2048,256]{1,2,0:T(8,128)(2,1)S(1)}, bf16[1,2048,256]{1,2,0:T(8,128)(2,1)}, u32[]{:S(2)}) copy-start(bf16[1,2048,256]{1,2,0:T(8,128)(2,1)} %copy.160) | copy-start | bytes 3145732 | tf_op jit(solution)/shard_map/while
  460.1 7.1 %copy-start.1 = (bf16[1,2048,256]{1,2,0:T(8,128)(2,1)S(1)}, bf16[1,2048,256]{1,2,0:T(8,128)(2,1)}, u32[]{:S(2)}) copy-start(bf16[1,2048,256]{1,2,0:T(8,128)(2,1)} %copy.160) | copy-start | bytes 3145732 | tf_op jit(solution)/shard_map/while
  490.3 7.1 %copy-start.1 = (bf16[1,2048,256]{1,2,0:T(8,128)(2,1)S(1)}, bf16[1,2048,256]{1,2,0:T(8,128)(2,1)}, u32[]{:S(2)}) copy-start(bf16[1,2048,256]{1,2,0:T(8,128)(2,1)} %copy.160) | copy-start | bytes 3145732 | tf_op jit(solution)/shard_map/while
  520.4 7.1 %copy-start.1 = (bf16[1,2048,256]{1,2,0:T(8,128)(2,1)S(1)}, bf16[1,2048,256]{1,2,0:T(8,128)(2,1)}, u32[]{:S(2)}) copy-start(bf16[1,2048,256]{1,2,0:T(8,128)(2,1)} %copy.160) | copy-start | bytes 3145732 | tf_op jit(solution)/shard_map/while
  550.6 7.1 %copy-start.1 = (bf16[1,2048,256]{1,2,0:T(8,128)(2,1)S(1)}, bf16[1,2048,256]{1,2,0:T(8,128)(2,1)}, u32[]{:S(2)}) copy-start(bf16[1,2048,256]{1,2,0:T(8,128)(2,1)} %copy.160) | copy-start | bytes 3145732 | tf_op jit(solution)/shard_map/while
  580.8 7.1 %copy-start.1 = (bf16[1,2048,256]{1,2,0:T(8,128)(2,1)S(1)}, bf16[1,2048,256]{1,2,0:T(8,128)(2,1)}, u32[]{:S(2)}) copy-start(bf16[1,2048,256]{1,2,0:T(8,128)(2,1)} %copy.160) | copy-start | bytes 3145732 | tf_op jit(solution)/shard_map/while
  611.0 7.1 %copy-start.1 = (bf16[1,2048,256]{1,2,0:T(8,128)(2,1)S(1)}, bf16[1,2048,256]{1,2,0:T(8,128)(2,1)}, u32[]{:S(2)}) copy-start(bf16[1,2048,256]{1,2,0:T(8,128)(2,1)} %copy.160) | copy-start | bytes 3145732 | tf_op jit(solution)/shard_map/while
  641.1 7.1 %copy-start.1 = (bf16[1,2048,256]{1,2,0:T(8,128)(2,1)S(1)}, bf16[1,2048,256]{1,2,0:T(8,128)(2,1)}, u32[]{:S(2)}) copy-start(bf16[1,2048,256]{1,2,0:T(8,128)(2,1)} %copy.160) | copy-start | bytes 3145732 | tf_op jit(solution)/shard_map/while
  666.2 4.9 copy-start.11
  666.2 4.9 copy-start.15
  672.9 1.6 copy-start.6
  672.9 1.6 copy-start.12
  672.9 1.6 copy-start.13
Sparse Core Ops, SparseCore 0:
  9.2 38.0 all-gather.10
  48.8 29.0 all-gather.14
  79.6 28.5 all-gather.16
  109.7 150.5 all-gather.12
  261.7 80.2 all-gather.8
  343.5 80.5 all-gather.6
where the time goes:
time: 687 us; the launch traced here: 686 us
  waiting for transfers between devices  374 us (54%)
  matrix products  133 us (19%)
  local copies, waits for them, and re-layouts  84.7 us (12%)
  other arithmetic  80.2 us (12%)
  between operations  13.9 us (2%)
    all_gather x1, waiting for transfers between devices, shards(): lax.all_gather(w_query, 'fsdp', axis=0, tiled=True)  150 us
    all_gather x1, waiting for transfers between devices, shards(): value_piece = lax.all_gather(value_cache, 'fsdp', axis=0, tiled=True)  82.1 us
    reduce_sum x9, other arithmetic, partial_attend(): total = jnp.sum(weights, axis=-1)  63 us
    dot_general x9, matrix products, partial_attend(): jnp.einsum('tkgl,lkd->tkgd', rounded, value_rows, preferred_element_type=...  61.1 us
    dot_general x9, matrix products, partial_attend(): jnp.einsum('tkgd,lkd->tkgl', grouped, key_rows, preferred_element_type=jn...  58.6 us
    all_gather x1, waiting for transfers between devices, shards(): key_piece = lax.all_gather(key_cache, 'fsdp', axis=0, tiled=True)  50.4 us
    dynamic_slice x32, local copies, waits for them, and re-layouts, shards(): lax.map(one_document, (slot_queries.reshape((count, CAP) + slot_queries.s...  37.3 us
    all_gather x1, waiting for transfers between devices, shards(): full_rows = lax.all_gather(inputs, 'corpus', axis=1, tiled=True)  31.9 us
  transfers between devices with their start and end apart: 6, of which 6 were waited for; matrix products, arithmetic and copies ran while one was open for 6% of the time, Pallas kernels for 0%

commit v1 on v0

--- a/solution.py
+++ b/solution.py
@@ -9,6 +9,28 @@
 EPS = 1e-06
 THETA = 1000000.0
 MASKED = -1e30
+
+
+def laid_out(pieces, dim):
+    pieces = jnp.moveaxis(pieces, 0, dim)
+    dims = pieces.shape
+    return pieces.reshape(*dims[:dim], dims[dim] * dims[dim + 1], *dims[dim + 2 :])
+
+
+def collect(x, axis, dim):
+    size = lax.axis_size(axis)
+    pairs = [(i, (i + 1) % size) for i in range(size)]
+    back = [(b, a) for a, b in pairs]
+    lower, upper = ([], [])
+    for step in range(size - 1):
+        if step % 2 == 0:
+            lower.append(lax.ppermute(lower[-1] if lower else x, axis, pairs))
+        else:
+            upper.append(lax.ppermute(upper[-1] if upper else x, axis, back))
+    parts = jnp.stack([*lower[::-1], x, *upper])
+    shift = lax.axis_index(axis) - len(lower)
+    parts = parts[(jnp.arange(size) - shift) % size]
+    return laid_out(parts, dim)
 
 
 def rope_tables(position, width):
@@ -96,11 +118,7 @@
 ):
     full_rows = lax.all_gather(inputs, "corpus", axis=1, tiled=True)
     normed = normalize(full_rows, norm_gain)
-    query_lin = jnp.dot(
-        normed,
-        lax.all_gather(w_query, "fsdp", axis=0, tiled=True),
-        preferred_element_type=jnp.float32,
-    )
+    query_lin = jnp.dot(normed, collect(w_query, "fsdp", 0), preferred_element_type=jnp.float32)
     key_lin = jnp.dot(
         normed,
         lax.all_gather(w_key, "fsdp", axis=0, tiled=True),

time: 687 us -> 567 us (0.83)
  waiting for transfers between devices: 374 us -> 260 us
  local copies, waits for them, and re-layouts: 84.7 us -> 128 us
  matrix products: 133 us -> 95.2 us
  other arithmetic: 80.2 us -> 56.7 us
  starting transfers between devices: 0.19 us -> 11.3 us
    ppermute x0 -> x7, waiting for transfers between devices: none -> 238 us  [the longest x4 238 us: collect(): lower.append(lax.ppermute(lower[-1] if lower else x, axis, pairs))]
    all_gather x1 -> x0, waiting for transfers between devices: 150 us -> none  [shards(): lax.all_gather(w_query, 'fsdp', axis=0, tiled=True)]
    all_gather x1, waiting for transfers between devices: 82.1 us -> 0.01 us  [shards(): value_piece = lax.all_gather(value_cache, 'fsdp', axis=0, tiled=True)]
    dot_general x9, matrix products: 58.6 us -> 23.9 us  [partial_attend(): jnp.einsum('tkgd,lkd->tkgl', grouped, key_rows, preferred_element_type=jn...]
    all_gather x1, waiting for transfers between devices: 31.9 us -> 0.02 us  [shards(): full_rows = lax.all_gather(inputs, 'corpus', axis=1, tiled=True)]
    reduce_sum x9, other arithmetic: 63 us -> 31.2 us  [partial_attend(): total = jnp.sum(weights, axis=-1)]
    all_gather x1, waiting for transfers between devices: 50.4 us -> 18.7 us  [shards(): key_piece = lax.all_gather(key_cache, 'fsdp', axis=0, tiled=True)]
    all_gather x1, waiting for transfers between devices: 28.5 us -> 0.02 us  [shards(): lax.all_gather(w_key, 'fsdp', axis=0, tiled=True)]
  transfers between devices with their start and end apart: 6 -> 12, of which waited for: 6 -> 5; matrix products, arithmetic and copies ran while one was open for 6% -> 14% of each run, Pallas kernels for 0% -> 0%
where the time goes in v1:
time: 567 us; the launch traced here: 566 us
  waiting for transfers between devices  260 us (46%)
  local copies, waits for them, and re-layouts  128 us (23%)
  matrix products  95.2 us (17%)
  other arithmetic  56.7 us (10%)
  between operations  13.7 us (2%)
  starting transfers between devices  11.3 us (2%)
    ppermute x4, waiting for transfers between devices, collect(): lower.append(lax.ppermute(lower[-1] if lower else x, axis, pairs))  238 us
    dot_general x9, matrix products, partial_attend(): jnp.einsum('tkgl,lkd->tkgd', rounded, value_rows, preferred_element_type=...  61 us
    reduce_sum x9, other arithmetic, partial_attend(): total = jnp.sum(weights, axis=-1)  31.2 us
    dynamic_slice x32, local copies, waits for them, and re-layouts, shards(): lax.map(one_document, (slot_queries.reshape((count, CAP) + slot_queries.s...  31 us
    dot_general x9, matrix products, partial_attend(): jnp.einsum('tkgd,lkd->tkgl', grouped, key_rows, preferred_element_type=jn...  23.9 us
    gather x3, local copies, waits for them, and re-layouts, collect(): parts = parts[(jnp.arange(size) - shift) % size]  23.7 us
    all_gather x1, waiting for transfers between devices, shards(): key_piece = lax.all_gather(key_cache, 'fsdp', axis=0, tiled=True)  18.7 us
    while x16, local copies, waits for them, and re-layouts  15.3 us
  transfers between devices with their start and end apart: 12, of which 5 were waited for; matrix products, arithmetic and copies ran while one was open for 14% of the time, Pallas kernels for 0%

profile of v1, /device:TPU:0, one launch (start us, length us, event | category | flops | bytes accessed | tf_op | source)
XLA Modules:
  0.0 565.7 jit_solution(3845225101653030087)
XLA Ops:
  9.9 27.9 %collective-permute-done = bf16[512,2048]{1,0:T(8,128)(2,1)} collective-permute-done((bf16[512,2048]{1,0:T(8,128)(2,1)S(1)}, bf16[512,2048]{1,0:T(8,128)(2,1)}, u32[]{:S(2)}, u32[]{:S(2)}) %collective-permute-start) | collective-permute-done | bytes 2097184 | tf_op jit(solution)/shard_map/ppermute | solution.py:27
  37.8 3.6 collective-permute-start.4
  41.4 62.7 %collective-permute-done.1 = bf16[512,2048]{1,0:T(8,128)(2,1)} collective-permute-done((bf16[512,2048]{1,0:T(8,128)(2,1)}, bf16[512,2048]{1,0:T(8,128)(2,1)}, u32[]{:S(2)}, u32[]{:S(2)}) %collective-permute-start.1) | collective-permute-done | bytes 2097184 | tf_op jit(solution)/shard_map/ppermute | solution.py:27
  108.2 3.6 collective-permute-start.5
  111.8 72.0 %collective-permute-done.2 = bf16[512,2048]{1,0:T(8,128)(2,1)} collective-permute-done((bf16[512,2048]{1,0:T(8,128)(2,1)}, bf16[512,2048]{1,0:T(8,128)(2,1)}, u32[]{:S(2)}, u32[]{:S(2)}) %collective-permute-start.2) | collective-permute-done | bytes 2097184 | tf_op jit(solution)/shard_map/ppermute | solution.py:27
  183.9 2.2 fusion.13
  186.2 2.4 convolution_add_fusion.2
  188.8 3.1 fusion.27
  192.1 3.5 collective-permute-start.6
  195.6 76.0 %collective-permute-done.3 = bf16[512,2048]{1,0:T(8,128)(2,1)} collective-permute-done((bf16[512,2048]{1,0:T(8,128)(2,1)}, bf16[512,2048]{1,0:T(8,128)(2,1)}, u32[]{:S(2)}, u32[]{:S(2)}) %collective-permute-start.3) | collective-permute-done | bytes 2097184 | tf_op jit(solution)/shard_map/ppermute | solution.py:27
  271.6 1.8 bitcast_dynamic-update-slice_fusion.9
  273.4 1.8 bitcast_dynamic-update-slice_fusion.8
  275.3 1.8 bitcast_dynamic-update-slice_fusion.7
  277.1 2.0 bitcast_dynamic-update-slice_fusion.6
  279.5 1.8 bitcast_dynamic-update-slice_fusion.4
  281.3 1.8 bitcast_dynamic-update-slice_fusion.3
  283.3 7.3 %fusion.58 = (bf16[8,512,1024]{2,1,0:T(8,128)(2,1)}, bf16[8,512,1024]{2,1,0:T(8,128)(2,1)}) fusion(bf16[8,512,2048]{2,1,0:T(8,128)(2,1)S(1)} %bitcast_dynamic-update-slice_fusion.2), kind=kLoop, calls=%fused_computation.123 | loop fusion | bytes 33554432 | tf_op jit(solution)/shard_map/gather | solution.py:32
  290.6 8.1 %gather_fusion.3 = bf16[8,512,1024]{2,1,0:T(8,128)(2,1)} fusion(bf16[8,512,1024]{2,1,0:T(8,128)(2,1)} %get-tuple-element.106, s32[1024]{0:T(1024)S(1)} %get-tuple-element.118), kind=kCustom, calls=%fused_computation.5 | custom fusion | bytes 16777248 | tf_op jit(solution)/shard_map/gather | solution.py:32
  298.7 8.3 %gather_fusion.4 = bf16[8,512,1024]{2,1,0:T(8,128)(2,1)} fusion(bf16[8,512,1024]{2,1,0:T(8,128)(2,1)} %get-tuple-element.107, s32[1024]{0:T(1024)S(1)} %get-tuple-element.118), kind=kCustom, calls=%fused_computation.6 | custom fusion | bytes 16777248 | tf_op jit(solution)/shard_map/gather | solution.py:32
  307.1 8.2 %pad_maximum_fusion = bf16[8,512,2048]{2,1,0:T(8,128)(2,1)S(1)} fusion(bf16[8,512,1024]{2,1,0:T(8,128)(2,1)} %gather_fusion.4, bf16[8,512,1024]{2,1,0:T(8,128)(2,1)} %gather_fusion.3), kind=kLoop, calls=%fused_computation.26 | loop fusion | flops 33554432 | bytes 33554432
  315.3 4.7 fusion.26
  323.8 1.7 fusion.59
  326.9 2.5 copy.105
  329.4 2.7 reshape.269
  332.2 2.9 fusion.20
  335.1 3.1 gather_fusion.1
  338.7 4.8 broadcast_select_fusion
  343.5 18.7 %all-gather.8.cloned.1.call-done = bf16[8,2048,256]{2,1,0:T(8,128)(2,1)} async-done(((bf16[1,2048,256]{2,1,0:T(8,128)(2,1)}), bf16[8,2048,256]{2,1,0:T(8,128)(2,1)}) %all-gather.8.cloned.1.call-update) | async-done | bytes 8388624 | tf_op jit(solution)/shard_map/all_gather | solution.py:174
  362.1 183.7 %while.14 = (s32[]{:T(128)}, f32[8,2,64,2048]{3,2,1,0:T(8,128)}, f32[8,2,64,16]{2,3,1,0:T(8,128)S(1)}, f32[8,2,64,16]{2,3,1,0:T(8,128)S(1)}, bf16[8,2048,256]{2,...) while((s32[]{:T(128)}, f32[8,2,64,2048]{3,2,1,0:T(8,128)}, ...), condition=%wide.region_7.8_spmd, body=%wide.region_4.7_spmd.sunk | while | flops 2193620992 | bytes 136962704 | solution.py:185
  362.2 1.3 constant_dynamic-slice_fusion.5
  365.2 2.8 fusion.74
  368.0 3.8 fusion.76
  371.8 1.9 copy-done
  375.7 7.6 %fusion.75 = f32[2,64,2,8,128]{4,1,3,0,2:T(8,128)S(1)} fusion(bf16[2048,2,128,1,1]{0,2,4,3,1:T(8,128)(2,1)S(1)} %bitcast.161, f32[2,2048,2,64,8]{1,3,4,2,0:T(8,128)} %copy-done, f32[2,64,2,8]{1,3,0,2:T(8,128)S(1)} %get-tuple-element.173, pred[2,2048]{1,0:T(4,128)(4,1)S(1)} %compare_bitcast_fusion.2), kind=kOutput, calls=%fused_computation.14.clone.1 | convolution fusion | flops 1090519040 | bytes 18886656 | tf_op jit(solution)/shard_map/while/body/eval_jaxpr/vmap(tkgl,lkd->tkgd)/dot_general | solution.py:73
  388.2 2.8 fusion.74
  390.9 3.8 fusion.76
  394.8 1.9 copy-done
  398.6 7.6 %fusion.75 = f32[2,64,2,8,128]{4,1,3,0,2:T(8,128)S(1)} fusion(bf16[2048,2,128,1,1]{0,2,4,3,1:T(8,128)(2,1)S(1)} %bitcast.161, f32[2,2048,2,64,8]{1,3,4,2,0:T(8,128)} %copy-done, f32[2,64,2,8]{1,3,0,2:T(8,128)S(1)} %get-tuple-element.173, pred[2,2048]{1,0:T(4,128)(4,1)S(1)} %compare_bitcast_fusion.2), kind=kOutput, calls=%fused_computation.14.clone.1 | convolution fusion | flops 1090519040 | bytes 18886656 | tf_op jit(solution)/shard_map/while/body/eval_jaxpr/vmap(tkgl,lkd->tkgd)/dot_general | solution.py:73
  411.1 2.8 fusion.74
  413.9 3.8 fusion.76
  417.7 1.9 copy-done
  421.6 7.6 %fusion.75 = f32[2,64,2,8,128]{4,1,3,0,2:T(8,128)S(1)} fusion(bf16[2048,2,128,1,1]{0,2,4,3,1:T(8,128)(2,1)S(1)} %bitcast.161, f32[2,2048,2,64,8]{1,3,4,2,0:T(8,128)} %copy-done, f32[2,64,2,8]{1,3,0,2:T(8,128)S(1)} %get-tuple-element.173, pred[2,2048]{1,0:T(4,128)(4,1)S(1)} %compare_bitcast_fusion.2), kind=kOutput, calls=%fused_computation.14.clone.1 | convolution fusion | flops 1090519040 | bytes 18886656 | tf_op jit(solution)/shard_map/while/body/eval_jaxpr/vmap(tkgl,lkd->tkgd)/dot_general | solution.py:73
  434.0 2.8 fusion.74
  436.8 3.8 fusion.76
  440.7 1.9 copy-done
  444.5 7.6 %fusion.75 = f32[2,64,2,8,128]{4,1,3,0,2:T(8,128)S(1)} fusion(bf16[2048,2,128,1,1]{0,2,4,3,1:T(8,128)(2,1)S(1)} %bitcast.161, f32[2,2048,2,64,8]{1,3,4,2,0:T(8,128)} %copy-done, f32[2,64,2,8]{1,3,0,2:T(8,128)S(1)} %get-tuple-element.173, pred[2,2048]{1,0:T(4,128)(4,1)S(1)} %compare_bitcast_fusion.2), kind=kOutput, calls=%fused_computation.14.clone.1 | convolution fusion | flops 1090519040 | bytes 18886656 | tf_op jit(solution)/shard_map/while/body/eval_jaxpr/vmap(tkgl,lkd->tkgd)/dot_general | solution.py:73
  457.0 2.8 fusion.74
  459.8 3.8 fusion.76
  463.6 1.9 copy-done
  467.5 7.6 %fusion.75 = f32[2,64,2,8,128]{4,1,3,0,2:T(8,128)S(1)} fusion(bf16[2048,2,128,1,1]{0,2,4,3,1:T(8,128)(2,1)S(1)} %bitcast.161, f32[2,2048,2,64,8]{1,3,4,2,0:T(8,128)} %copy-done, f32[2,64,2,8]{1,3,0,2:T(8,128)S(1)} %get-tuple-element.173, pred[2,2048]{1,0:T(4,128)(4,1)S(1)} %compare_bitcast_fusion.2), kind=kOutput, calls=%fused_computation.14.clone.1 | convolution fusion | flops 1090519040 | bytes 18886656 | tf_op jit(solution)/shard_map/while/body/eval_jaxpr/vmap(tkgl,lkd->tkgd)/dot_general | solution.py:73
  480.0 2.8 fusion.74
  482.7 3.8 fusion.76
  486.6 1.9 copy-done
  490.4 7.6 %fusion.75 = f32[2,64,2,8,128]{4,1,3,0,2:T(8,128)S(1)} fusion(bf16[2048,2,128,1,1]{0,2,4,3,1:T(8,128)(2,1)S(1)} %bitcast.161, f32[2,2048,2,64,8]{1,3,4,2,0:T(8,128)} %copy-done, f32[2,64,2,8]{1,3,0,2:T(8,128)S(1)} %get-tuple-element.173, pred[2,2048]{1,0:T(4,128)(4,1)S(1)} %compare_bitcast_fusion.2), kind=kOutput, calls=%fused_computation.14.clone.1 | convolution fusion | flops 1090519040 | bytes 18886656 | tf_op jit(solution)/shard_map/while/body/eval_jaxpr/vmap(tkgl,lkd->tkgd)/dot_general | solution.py:73
  502.9 2.8 fusion.74
  505.7 3.8 fusion.76
  509.6 1.9 copy-done
  513.4 7.6 %fusion.75 = f32[2,64,2,8,128]{4,1,3,0,2:T(8,128)S(1)} fusion(bf16[2048,2,128,1,1]{0,2,4,3,1:T(8,128)(2,1)S(1)} %bitcast.161, f32[2,2048,2,64,8]{1,3,4,2,0:T(8,128)} %copy-done, f32[2,64,2,8]{1,3,0,2:T(8,128)S(1)} %get-tuple-element.173, pred[2,2048]{1,0:T(4,128)(4,1)S(1)} %compare_bitcast_fusion.2), kind=kOutput, calls=%fused_computation.14.clone.1 | convolution fusion | flops 1090519040 | bytes 18886656 | tf_op jit(solution)/shard_map/while/body/eval_jaxpr/vmap(tkgl,lkd->tkgd)/dot_general | solution.py:73
  525.9 2.8 fusion.74
  528.7 3.8 fusion.76
  532.5 1.9 copy-done
  536.4 7.6 %fusion.75 = f32[2,64,2,8,128]{4,1,3,0,2:T(8,128)S(1)} fusion(bf16[2048,2,128,1,1]{0,2,4,3,1:T(8,128)(2,1)S(1)} %bitcast.161, f32[2,2048,2,64,8]{1,3,4,2,0:T(8,128)} %copy-done, f32[2,64,2,8]{1,3,0,2:T(8,128)S(1)} %get-tuple-element.173, pred[2,2048]{1,0:T(4,128)(4,1)S(1)} %compare_bitcast_fusion.2), kind=kOutput, calls=%fused_computation.14.clone.1 | convolution fusion | flops 1090519040 | bytes 18886656 | tf_op jit(solution)/shard_map/while/body/eval_jaxpr/vmap(tkgl,lkd->tkgd)/dot_general | solution.py:73
  547.7 4.2 gather_fusion.2
  554.7 4.4 fusion.16
  (205 shorter events, 71.8 us)
Async XLA Ops:
  6.5 2.9 copy-start.7
  6.5 97.5 %copy-start.19 = (s32[4]{0:T(128)S(1)}, s32[4]{0:T(128)}, u32[]{:S(2)}) copy-start(s32[4]{0:T(128)} %param.26) | copy-start | bytes 52
  6.5 97.9 %copy-start.1 = (s32[4]{0:T(128)S(1)}, s32[4]{0:T(128)}, u32[]{:S(2)}) copy-start(s32[4]{0:T(128)} %param.27) | copy-start | bytes 52
  6.5 177.4 %all-gather.10.cloned.1.call-start = ((), (), s32[]{:S(2)}) async-start(), calls=%async_computation.2 | async-start | bytes 2621440 | tf_op jit(solution)/shard_map/all_gather | solution.py:119
  7.3 178.9 %all-gather.12.cloned.1.call-start = ((), (), s32[]{:S(2)}) async-start(), calls=%async_computation.3 | async-start | bytes 2359296 | tf_op jit(solution)/shard_map/all_gather | solution.py:124
  8.0 180.8 %all-gather.14.cloned.1.call-start = ((), (), s32[]{:S(2)}) async-start(), calls=%async_computation.4 | async-start | bytes 2359296 | tf_op jit(solution)/shard_map/all_gather | solution.py:129
  8.7 334.7 %all-gather.6.cloned.1.call-start = ((), (), s32[]{:S(2)}) async-start(), calls=%async_computation | async-start | bytes 9437184 | tf_op jit(solution)/shard_map/all_gather | solution.py:175
  9.3 176.9 %copy-start.20 = (f32[4096]{0:T(1024)S(1)}, f32[4096]{0:T(1024)}, u32[]{:S(2)}) copy-start(f32[4096]{0:T(1024)} %param.17) | copy-start | bytes 49156
  9.3 176.9 %copy-start.22 = (f32[256]{0:T(256)S(1)}, f32[256]{0:T(256)}, u32[]{:S(2)}) copy-start(f32[256]{0:T(256)} %param.22) | copy-start | bytes 3076
  9.3 352.8 %all-gather.8.cloned.1.call-start = ((), (), s32[]{:S(2)}) async-start(), calls=%async_computation.1 | async-start | bytes 9437184 | tf_op jit(solution)/shard_map/all_gather | solution.py:174
  9.4 28.4 %collective-permute-start = (bf16[512,2048]{1,0:T(8,128)(2,1)S(1)}, bf16[512,2048]{1,0:T(8,128)(2,1)}, u32[]{:S(2)}, u32[]{:S(2)}) collective-permute-start(bf16[512,2048]{1,0:T(8,128)(2,1)S(1)} %copy-done.7), channel_id=1, source_target_pairs={{0,1},{1,2},{2,3},{3,4},{4,5},{5,6},{6,7},{7,0},{8,9},{9,10},{10,1... | collective-permute-start | bytes 6291464 | tf_op jit(solution)/shard_map/ppermute | solution.py:27
  37.8 66.3 %collective-permute-start.1 = (bf16[512,2048]{1,0:T(8,128)(2,1)}, bf16[512,2048]{1,0:T(8,128)(2,1)}, u32[]{:S(2)}, u32[]{:S(2)}) collective-permute-start(bf16[512,2048]{1,0:T(8,128)(2,1)} %collective-permute-done), channel_id=1, source_target_pairs={{0,1},{1,2},{2,3},{3,4},{4,5},{5,6},{6,7},{7,0},{8,9},{9,10},{10,1... | collective-permute-start | bytes 6291464 | tf_op jit(solution)/shard_map/ppermute | solution.py:27
  37.8 70.4 %collective-permute-start.4 = (bf16[512,2048]{1,0:T(8,128)(2,1)S(1)}, bf16[512,2048]{1,0:T(8,128)(2,1)}, u32[]{:S(2)}, u32[]{:S(2)}) collective-permute-start(bf16[512,2048]{1,0:T(8,128)(2,1)S(1)} %copy-done.7), channel_id=1, source_target_pairs={{1,0},{2,1},{3,2},{4,3},{5,4},{6,5},{7,6},{0,7},{9,8},{10,9},{11,1... | collective-permute-start | bytes 6291464 | tf_op jit(solution)/shard_map/ppermute | solution.py:29
  104.0 79.7 %collective-permute-start.2 = (bf16[512,2048]{1,0:T(8,128)(2,1)}, bf16[512,2048]{1,0:T(8,128)(2,1)}, u32[]{:S(2)}, u32[]{:S(2)}) collective-permute-start(bf16[512,2048]{1,0:T(8,128)(2,1)} %collective-permute-done.1), channel_id=1, source_target_pairs={{0,1},{1,2},{2,3},{3,4},{4,5},{5,6},{6,7},{7,0},{8,9},{9,10},{10,1... | collective-permute-start | bytes 6291464 | tf_op jit(solution)/shard_map/ppermute | solution.py:27
  104.2 2.6 copy-start.13
  105.4 1.4 copy-start.17
  108.2 84.0 %collective-permute-start.5 = (bf16[512,2048]{1,0:T(8,128)(2,1)}, bf16[512,2048]{1,0:T(8,128)(2,1)}, u32[]{:S(2)}, u32[]{:S(2)}) collective-permute-start(bf16[512,2048]{1,0:T(8,128)(2,1)} %collective-permute-done.4), channel_id=1, source_target_pairs={{1,0},{2,1},{3,2},{4,3},{5,4},{6,5},{7,6},{0,7},{9,8},{10,9},{11,1... | collective-permute-start | bytes 6291464 | tf_op jit(solution)/shard_map/ppermute | solution.py:29
  183.7 87.9 %collective-permute-start.3 = (bf16[512,2048]{1,0:T(8,128)(2,1)}, bf16[512,2048]{1,0:T(8,128)(2,1)}, u32[]{:S(2)}, u32[]{:S(2)}) collective-permute-start(bf16[512,2048]{1,0:T(8,128)(2,1)} %collective-permute-done.2), channel_id=1, source_target_pairs={{0,1},{1,2},{2,3},{3,4},{4,5},{5,6},{6,7},{7,0},{8,9},{9,10},{10,1... | collective-permute-start | bytes 6291464 | tf_op jit(solution)/shard_map/ppermute | solution.py:27
  183.9 2.3 copy-start.9
  186.2 2.6 copy-start.23
  192.1 91.0 %collective-permute-start.6 = (bf16[512,2048]{1,0:T(8,128)(2,1)}, bf16[512,2048]{1,0:T(8,128)(2,1)S(1)}, u32[]{:S(2)}, u32[]{:S(2)}) collective-permute-start(bf16[512,2048]{1,0:T(8,128)(2,1)} %collective-permute-done.5), channel_id=1, source_target_pairs={{1,0},{2,1},{3,2},{4,3},{5,4},{6,5},{7,6},{0,7},{9,8},{10,9},{11,1... | collective-permute-start | bytes 6291464 | tf_op jit(solution)/shard_map/ppermute | solution.py:29
  277.1 2.2 copy-start.8
  307.1 8.2 %copy-start.10 = (bf16[256,4096]{1,0:T(8,128)(2,1)S(1)}, bf16[256,4096]{1,0:T(8,128)(2,1)}, u32[]{:S(2)}) copy-start(bf16[256,4096]{1,0:T(8,128)(2,1)} %all-gather.10.cloned.1.call-done) | copy-start | bytes 6291460
  307.1 8.2 %copy-start.21 = (f32[2048]{0:T(1024)S(1)}, f32[2048]{0:T(1024)}, u32[]{:S(2)}) copy-start(f32[2048]{0:T(1024)} %param.21) | copy-start | bytes 24580
  321.1 1.3 copy-start.4
  321.1 2.0 copy-start.5
  325.5 1.4 copy-start.2
  335.1 3.1 copy-start.3
  338.7 23.4 %copy-start.11 = (f32[8,2,64,16]{2,3,1,0:T(8,128)S(1)}, f32[8,2,64,16]{2,3,1,0:T(8,128)}, u32[]{:S(2)}) copy-start(f32[8,2,64,16]{2,3,1,0:T(8,128)} %custom-call.16) | copy-start | bytes 196612
  338.7 23.4 %copy-start.12 = (f32[8,2,64,16]{2,3,1,0:T(8,128)S(1)}, f32[8,2,64,16]{2,3,1,0:T(8,128)}, u32[]{:S(2)}) copy-start(f32[8,2,64,16]{2,3,1,0:T(8,128)} %custom-call.17) | copy-start | bytes 196612
  362.1 185.1 %copy-start.14 = (pred[4]{0:T(512)(128)(4,1)S(1)}, pred[4]{0:T(512)(128)(4,1)}, u32[]{:S(2)}) copy-start(pred[4]{0:T(512)(128)(4,1)} %copy-done.13) | copy-start | bytes 16
  362.1 185.1 %copy-start.18 = (pred[4]{0:T(512)(128)(4,1)S(1)}, pred[4]{0:T(512)(128)(4,1)}, u32[]{:S(2)}) copy-start(pred[4]{0:T(512)(128)(4,1)} %copy-done.17) | copy-start | bytes 16
  368.0 5.8 %copy-start = (f32[2,2048,2,64,8]{1,3,4,2,0:T(8,128)}, f32[2,2048,2,64,8]{1,3,4,2,0:T(8,128)S(1)}, u32[]{:S(2)}) copy-start(f32[2,2048,2,64,8]{1,3,4,2,0:T(8,128)S(1)} %get-tuple-element.172) | copy-start | bytes 50331652 | tf_op jit(solution)/shard_map/while
  390.9 5.8 %copy-start = (f32[2,2048,2,64,8]{1,3,4,2,0:T(8,128)}, f32[2,2048,2,64,8]{1,3,4,2,0:T(8,128)S(1)}, u32[]{:S(2)}) copy-start(f32[2,2048,2,64,8]{1,3,4,2,0:T(8,128)S(1)} %get-tuple-element.172) | copy-start | bytes 50331652 | tf_op jit(solution)/shard_map/while
  413.9 5.8 %copy-start = (f32[2,2048,2,64,8]{1,3,4,2,0:T(8,128)}, f32[2,2048,2,64,8]{1,3,4,2,0:T(8,128)S(1)}, u32[]{:S(2)}) copy-start(f32[2,2048,2,64,8]{1,3,4,2,0:T(8,128)S(1)} %get-tuple-element.172) | copy-start | bytes 50331652 | tf_op jit(solution)/shard_map/while
  436.8 5.8 %copy-start = (f32[2,2048,2,64,8]{1,3,4,2,0:T(8,128)}, f32[2,2048,2,64,8]{1,3,4,2,0:T(8,128)S(1)}, u32[]{:S(2)}) copy-start(f32[2,2048,2,64,8]{1,3,4,2,0:T(8,128)S(1)} %get-tuple-element.172) | copy-start | bytes 50331652 | tf_op jit(solution)/shard_map/while
  459.8 5.8 %copy-start = (f32[2,2048,2,64,8]{1,3,4,2,0:T(8,128)}, f32[2,2048,2,64,8]{1,3,4,2,0:T(8,128)S(1)}, u32[]{:S(2)}) copy-start(f32[2,2048,2,64,8]{1,3,4,2,0:T(8,128)S(1)} %get-tuple-element.172) | copy-start | bytes 50331652 | tf_op jit(solution)/shard_map/while
  482.7 5.8 %copy-start = (f32[2,2048,2,64,8]{1,3,4,2,0:T(8,128)}, f32[2,2048,2,64,8]{1,3,4,2,0:T(8,128)S(1)}, u32[]{:S(2)}) copy-start(f32[2,2048,2,64,8]{1,3,4,2,0:T(8,128)S(1)} %get-tuple-element.172) | copy-start | bytes 50331652 | tf_op jit(solution)/shard_map/while
  505.7 5.8 %copy-start = (f32[2,2048,2,64,8]{1,3,4,2,0:T(8,128)}, f32[2,2048,2,64,8]{1,3,4,2,0:T(8,128)S(1)}, u32[]{:S(2)}) copy-start(f32[2,2048,2,64,8]{1,3,4,2,0:T(8,128)S(1)} %get-tuple-element.172) | copy-start | bytes 50331652 | tf_op jit(solution)/shard_map/while
  528.6 5.8 %copy-start = (f32[2,2048,2,64,8]{1,3,4,2,0:T(8,128)}, f32[2,2048,2,64,8]{1,3,4,2,0:T(8,128)S(1)}, u32[]{:S(2)}) copy-start(f32[2,2048,2,64,8]{1,3,4,2,0:T(8,128)S(1)} %get-tuple-element.172) | copy-start | bytes 50331652 | tf_op jit(solution)/shard_map/while
  553.1 1.6 copy-start.6
  553.1 1.6 copy-start.15
  553.1 1.6 copy-start.16
Sparse Core Ops, SparseCore 0:
  9.2 38.0 all-gather.9
  48.9 41.9 all-gather.11
  92.5 43.0 all-gather.13
  137.0 136.1 all-gather.5
  274.6 87.4 all-gather.7
